TPU v7x, 32 devices: a whole 2x2x4 slice. The times are simulated.
32 devices in a mesh: dp: 8 (over z, y), own: 4 (over x, core).
Axes of the slice: x: 2, y: 2, z: 4, core: 2. Of those that a mesh axis runs over, the one named last changes fastest.
Arguments:
- acts_kv: bfloat16 [1024, 2560], P('dp', 'own'), may hold values from -6 to 6
- grads_kv: bfloat16 [1024, 1024], P('dp', 'own'), may hold values from -6 to 6
- acts_up: bfloat16 [1024, 2560], P('dp', 'own'), may hold values from -6 to 6
- grads_up: bfloat16 [1024, 3072], P('dp', 'own'), may hold values from -6 to 6
- prev_a_kv: float32 [4, 640, 640], P('own'), as said below
- prev_g_kv: float32 [4, 256, 256], P('own'), as said below
- prev_a_up: float32 [4, 640, 640], P('own'), as said below
- prev_g_up: float32 [4, 768, 768], P('own'), as said below
- owners: int32 [2, 4], replicated, may hold values from 0 to 7, as said below
- damping: float32 [4], replicated, may hold values from 0.05 to 0.5
- init_scale: float32 [4, 4], replicated, may hold values from 0.4 to 0.8
- weights_kv: float32 [2560, 1024], P('own', 'dp'), may hold values from -0.75 to 0.75
- weights_up: float32 [2560, 3072], P('own', 'dp'), may hold values from -0.75 to 0.75
- step_size: float32 [], replicated, may hold values from 0.2 to 0.5
Outputs:
- new_kv: float32 [2560, 1024], P('own', 'dp')
- new_up: float32 [2560, 3072], P('own', 'dp')
Inputs may be any that keep to these rules, and one draw needn't show every extreme that they name: `owners`: row 0 names for each factor the dp index that inverts it: one index is named by two factors, the others by one, and 0 and 7 are always named. Row 1 refreshes both factors of one of the two linears and leaves at least one factor of the other unrefreshed. `prev_a_kv`: every block is symmetric and positive definite. `prev_g_kv`: every block is symmetric and positive definite. `prev_a_up`: every block is symmetric and positive definite. `prev_g_up`: every block is symmetric and positive definite.
All inputs are finite; a program needn't handle non-finite values.
Results may differ from a plain program's by a relative error of at most 0.0021.
Values may be sent and summed in bfloat16 or wider, within the bound.
No kernel may reach another device: no remote copies, remote signals or barrier semaphores. Data moves between devices by JAX's collectives and lax.ppermute only.
A program may use at most 128 MiB of HBM per device.

v0:
```python
import jax
import jax.numpy as jnp
from jax import lax
from jax.sharding import PartitionSpec as P

D = 2560
OUT_KV = 1024
OUT_UP = 3072
NF = 4
NS_STEPS = 2


def spread(value, axis, root):
    mine = lax.axis_index(axis) == root
    return lax.psum(jnp.where(mine, value, jnp.zeros_like(value)), axis)


def matrix_product(left_side, right_side):
    return jnp.dot(
        left_side, right_side, preferred_element_type=jnp.float32, precision=lax.Precision.HIGHEST
    )


def outer_sum(values):
    return lax.dot_general(
        values, values, (((0,), (0,)), ((), ())), preferred_element_type=jnp.float32
    )


def blend_factor(previous, summed, fresh, damping_value, identity):
    return jnp.where(fresh == 1, 0.5 * previous + 0.5 * summed, previous) + damping_value * identity


def newton_schulz(damped, scale_value):
    block_width = damped.shape[0]
    identity = jnp.eye(block_width, dtype=jnp.float32)
    frobenius = jnp.sqrt(jnp.sum(damped * damped))
    iterate = scale_value / frobenius * identity
    for repeat in range(NS_STEPS):
        iterate = 2.0 * iterate - matrix_product(matrix_product(damped, iterate), iterate)
    return iterate.astype(jnp.bfloat16)


def apply_output_inverse(grad_low, blocks):
    block_count, block_width, unused = blocks.shape
    shaped = grad_low.reshape(grad_low.shape[0], block_count, block_width)
    product = jnp.einsum("rjb,jbc->rjc", shaped, blocks, preferred_element_type=jnp.float32)
    return product.reshape(grad_low.shape).astype(jnp.bfloat16)


def shards(
    acts_kv,
    grads_kv,
    acts_up,
    grads_up,
    prev_a_kv,
    prev_g_kv,
    prev_a_up,
    prev_g_up,
    owners,
    damping,
    init_scale,
    weights_kv,
    weights_up,
    step_size,
):
    dp_count = lax.axis_size("dp")
    dp_index = lax.axis_index("dp")
    own_index = lax.axis_index("own")
    total_tokens = acts_kv.shape[0] * dp_count
    full_kv, full_up = (
        lax.all_gather(grads_kv, "own", axis=1, tiled=True),
        lax.all_gather(grads_up, "own", axis=1, tiled=True),
    )
    column_block = acts_kv
    gradient_kv = (
        lax.psum_scatter(
            lax.dot_general(
                column_block, full_kv, (((0,), (0,)), ((), ())), preferred_element_type=jnp.float32
            ),
            "dp",
            scatter_dimension=0,
            tiled=True,
        )
        / total_tokens
    )
    column_block = acts_up
    gradient_up = (
        lax.psum_scatter(
            lax.dot_general(
                column_block, full_up, (((0,), (0,)), ((), ())), preferred_element_type=jnp.float32
            ),
            "dp",
            scatter_dimension=0,
            tiled=True,
        )
        / total_tokens
    )
    partials = (outer_sum(acts_kv), outer_sum(grads_kv), outer_sum(acts_up), outer_sum(grads_up))
    previous = (prev_a_kv[0], prev_g_kv[0], prev_a_up[0], prev_g_up[0])
    scales = lax.dynamic_index_in_dim(init_scale, own_index, 1, keepdims=False)
    summed_rows = (
        lax.psum_scatter(partials[0], "dp", scatter_dimension=0, tiled=True),
        lax.psum_scatter(partials[1], "dp", scatter_dimension=0, tiled=True),
        lax.psum_scatter(partials[2], "dp", scatter_dimension=0, tiled=True),
        lax.psum_scatter(partials[3], "dp", scatter_dimension=0, tiled=True),
    )
    summed = (
        lax.all_gather(summed_rows[0], "dp", axis=0, tiled=True),
        lax.all_gather(summed_rows[1], "dp", axis=0, tiled=True),
        lax.all_gather(summed_rows[2], "dp", axis=0, tiled=True),
        lax.all_gather(summed_rows[3], "dp", axis=0, tiled=True),
    )
    inverses = []
    for factor in range(NF):
        owner_index = owners[0, factor]
        identity = jnp.eye(previous[factor].shape[0], dtype=jnp.float32)
        damped = blend_factor(
            previous[factor],
            summed[factor] / total_tokens,
            owners[1, factor],
            damping[factor],
            identity,
        )
        local_inverse = lax.cond(
            dp_index == owner_index,
            lambda matrix: newton_schulz(matrix, scales[factor]),
            lambda matrix: jnp.zeros(matrix.shape, jnp.bfloat16),
            damped,
        )
        inverses.append(spread(local_inverse, "dp", owner_index))
    blocks_kv, blocks_up = (
        lax.all_gather(inverses[1][None], "own", axis=0, tiled=True),
        lax.all_gather(inverses[3][None], "own", axis=0, tiled=True),
    )
    low_kv = gradient_kv.astype(jnp.bfloat16)
    low_up = gradient_up.astype(jnp.bfloat16)
    right_kv = apply_output_inverse(low_kv, blocks_kv)
    right_up = apply_output_inverse(low_up, blocks_up)
    arrived = (
        lax.all_to_all(right_kv, "dp", split_axis=1, concat_axis=0, tiled=True),
        lax.all_to_all(low_kv, "dp", split_axis=1, concat_axis=0, tiled=True),
        lax.all_to_all(right_up, "dp", split_axis=1, concat_axis=0, tiled=True),
        lax.all_to_all(low_up, "dp", split_axis=1, concat_axis=0, tiled=True),
    )
    precond_kv = jnp.dot(inverses[0], arrived[0], preferred_element_type=jnp.float32)
    precond_up = jnp.dot(inverses[2], arrived[2], preferred_element_type=jnp.float32)
    term_kv = jnp.sum(precond_kv * arrived[1].astype(jnp.float32))
    term_up = jnp.sum(precond_up * arrived[3].astype(jnp.float32))
    totals = lax.psum((term_kv, term_up), ("dp", "own"))
    new_kv = weights_kv - step_size * jnp.sqrt(D * OUT_KV / totals[0]) * precond_kv
    new_up = weights_up - step_size * jnp.sqrt(D * OUT_UP / totals[1]) * precond_up
    return (new_kv, new_up)


def solution(mesh):
    return jax.shard_map(
        shards,
        mesh=mesh,
        in_specs=(
            P("dp", "own"),
            P("dp", "own"),
            P("dp", "own"),
            P("dp", "own"),
            P("own", None, None),
            P("own", None, None),
            P("own", None, None),
            P("own", None, None),
            P(),
            P(),
            P(),
            P("own", "dp"),
            P("own", "dp"),
            P(),
        ),
        out_specs=(P("own", "dp"), P("own", "dp")),
        check_vma=False,
    )
```

profile of v0, /device:TPU:0, one launch (start us, length us, event | category | flops | bytes accessed | tf_op | source)
XLA Modules:
  0.0 931.1 jit_solution(16209690147066611134)
XLA Ops:
  7.2 2.6 fusion.74
  15.4 64.0 %reduce-scatter.7.cloned.1.call-done = f32[80,640]{1,0:T(8,128)} async-done(((f32[640,640]{1,0:T(8,128)}), f32[80,640]{1,0:T(8,128)}) %reduce-scatter.7.cloned.1.call-update) | async-done | bytes 204816 | tf_op jit(solution)/shard_map/reduce_scatter | solution.py:103
  79.5 68.1 %reduce-scatter.13.cloned.1.call-done = f32[80,640]{1,0:T(8,128)} async-done(((f32[640,640]{1,0:T(8,128)}), f32[80,640]{1,0:T(8,128)}) %reduce-scatter.13.cloned.1.call-update) | async-done | bytes 204816 | tf_op jit(solution)/shard_map/reduce_scatter | solution.py:105
  147.7 71.4 %reduce-scatter.15.cloned.1.call-done = f32[96,768]{1,0:T(8,128)} async-done(((f32[768,768]{1,0:T(8,128)}), f32[96,768]{1,0:T(8,128)}) %reduce-scatter.15.cloned.1.call-update) | async-done | bytes 294928 | tf_op jit(solution)/shard_map/reduce_scatter | solution.py:106
  223.3 59.8 %reduce-scatter.9.cloned.1.call-done = f32[32,256]{1,0:T(8,128)} async-done(((f32[256,256]{1,0:T(8,128)}), f32[32,256]{1,0:T(8,128)}) %reduce-scatter.9.cloned.1.call-update) | async-done | bytes 32784 | tf_op jit(solution)/shard_map/reduce_scatter | solution.py:104
  283.1 31.2 %all_gather.25 = f32[256,256]{1,0:T(8,128)S(1)} all-gather(f32[32,256]{1,0:T(8,128)} %reduce-scatter.9.cloned.1.call-done), channel_id=1, replica_groups=mesh['dp'=8,'own'=4] {'dp'}, dimensions={0}, use_global_device_ids=true | all-gather | bytes 294912 | tf_op jit(solution)/shard_map/all_gather | solution.py:110
  315.1 14.2 %all-gather.5.cloned.1.call-done = f32[640,640]{1,0:T(8,128)} async-done(((f32[80,640]{1,0:T(8,128)}), f32[640,640]{1,0:T(8,128)}) %all-gather.5.cloned.1.call-update) | async-done | bytes 1638416 | tf_op jit(solution)/shard_map/all_gather | solution.py:109
  332.0 29.4 %conditional.4 = (bf16[640,640]{1,0:T(8,128)(2,1)S(1)}) conditional(s32[]{:T(128)} %convert_element_type.80, () %tuple.44, (f32[4]{0:T(128)S(1)}, s32[2,4]{1,0:T(2,128)S(1)}, f32[1,640,640]{2,1,0:T(8,128)}, f32[640,640]{1,0:T(8,128)S(1)}, f32[640,640]{1,0:T(8,128)}, /*index=5*/f32[640,640]{1,0:T(8,128)}, f32[4]{0:T(128)S(1)}, ...), branch_computations={%region_1.0_spmd, %region_2.0_spmd} | conditional | flops 12590694400 | bytes 25804862 | solution.py:125
  333.7 4.2 multiply_reduce_fusion
  338.6 4.6 fusion.2
  343.2 4.7 fusion.4
  347.9 8.2 fusion.70
  356.2 5.0 subtract_convert_fusion
  361.4 13.5 %all-gather.7.cloned.1.call-done = f32[640,640]{1,0:T(8,128)} async-done(((f32[80,640]{1,0:T(8,128)}), f32[640,640]{1,0:T(8,128)}) %all-gather.7.cloned.1.call-update) | async-done | bytes 1638416 | tf_op jit(solution)/shard_map/all_gather | solution.py:111
  374.9 9.3 conditional.6
  386.7 41.4 %all-gather.9.cloned.1.call-done = f32[768,768]{1,0:T(8,128)} async-done(((f32[96,768]{1,0:T(8,128)}), f32[768,768]{1,0:T(8,128)}) %all-gather.9.cloned.1.call-update) | async-done | bytes 2359312 | tf_op jit(solution)/shard_map/all_gather | solution.py:112
  431.3 5.4 conditional.7
  438.0 5.8 all_gather.27
  446.7 8.7 all_gather.31
  455.4 4.3 fusion.79
  459.8 136.7 %all-reduce.4.cloned.1.call-done = (bf16[640,640]{1,0:T(8,128)(2,1)}, bf16[1,256,256]{2,1,0:T(8,128)(2,1)}, bf16[640,640]{1,0:T(8,128)(2,1)}, bf16[1,768,768]{2,1,0:T(8,128)(2,1)}) async-done(((bf16[640,640]{1,0:T(8,128)(2,1)}, bf16[1,256,256]{2,1,0:T(8,128)(2,1)}, bf16[640,640]{1,0:T(8,128)(2,1)}, bf16[1,768,768]{2,1,0:T(8,128)(2,1)}), (bf16[640,640]{1,0:T(8,128)(2,1)}, bf16[1,256,256]{2,1,0:T(8,128)(2,1)}, ...) | async-done | bytes 2949136 | tf_op jit(solution)/shard_map/psum | solution.py:15
  596.5 73.3 %reduce-scatter.11.cloned.1.call-done = f32[80,1024]{1,0:T(8,128)} async-done(((f32[640,1024]{1,0:T(8,128)}), f32[80,1024]{1,0:T(8,128)}) %reduce-scatter.11.cloned.1.call-update) | async-done | bytes 327696 | tf_op jit(solution)/shard_map/reduce_scatter | solution.py:77
  671.5 3.5 all-to-all-start.1
  676.0 7.1 all_gather.26
  684.2 6.0 all-to-all-start
  690.2 126.9 %reduce-scatter.17.cloned.1.call-done = f32[80,3072]{1,0:T(8,128)} async-done(((f32[640,3072]{1,0:T(8,128)}), f32[80,3072]{1,0:T(8,128)}) %reduce-scatter.17.cloned.1.call-update) | async-done | bytes 983056 | tf_op jit(solution)/shard_map/reduce_scatter | solution.py:89
  819.2 3.7 all-to-all-start.3
  822.9 32.4 %all-gather.11.cloned.1.call-done = bf16[4,768,768]{2,1,0:T(8,128)(2,1)} async-done(((bf16[1,768,768]{2,1,0:T(8,128)(2,1)}), bf16[4,768,768]{2,1,0:T(8,128)(2,1)}) %all-gather.11.cloned.1.call-update) | async-done | bytes 4718608 | tf_op jit(solution)/shard_map/all_gather | solution.py:134
  855.4 3.2 fusion.57
  859.9 5.5 all-to-all-start.2
  867.0 12.5 %all-to-all-done.2 = bf16[80,8,384]{2,0,1:T(8,128)(2,1)S(1)} async-done(((bf16[80,8,384]{2,0,1:T(8,128)(2,1)}), bf16[80,8,384]{2,0,1:T(8,128)(2,1)S(1)}, u32[]{:S(2)}, u32[]{:S(2)}) %all-to-all-start.2) | async-done | bytes 491552 | tf_op jit(solution)/shard_map/all_to_all | solution.py:143
  882.1 38.8 %all-reduce = (f32[]{:T(128)}, f32[]{:T(128)}) all-reduce(f32[]{:T(128)} %get-tuple-element.298, f32[]{:T(128)} %get-tuple-element.300), channel_id=1, replica_groups=mesh['dp'=8,'own'=4] {'dp','own'}, use_global_device_ids=true, to_apply=%region_12.13 | all-reduce | flops 2 | bytes 16 | tf_op jit(solution)/shard_map/psum | solution.py:150
  (94 shorter events, 33.8 us)
Async XLA Ops:
  7.2 2.8 copy-start
  7.2 72.2 %reduce-scatter.7.cloned.1.call-start = ((), (), s32[]{:S(2)}) async-start(), calls=%async_computation.10 | async-start | bytes 1843200 | tf_op jit(solution)/shard_map/reduce_scatter | solution.py:103
  9.9 1.7 copy-start.2
  9.9 137.7 %reduce-scatter.13.cloned.1.call-start = ((), (), s32[]{:S(2)}) async-start(), calls=%async_computation.14 | async-start | bytes 1843200 | tf_op jit(solution)/shard_map/reduce_scatter | solution.py:105
  11.6 207.5 %reduce-scatter.15.cloned.1.call-start = ((), (), s32[]{:S(2)}) async-start(), calls=%async_computation.16 | async-start | bytes 2654208 | tf_op jit(solution)/shard_map/reduce_scatter | solution.py:106
  13.5 0.8 copy-start.9
  13.5 205.6 %copy-start.13 = (s32[2,4]{1,0:T(2,128)S(1)}, s32[2,4]{1,0:T(2,128)}, u32[]{:S(2)}) copy-start(s32[2,4]{1,0:T(2,128)} %param.30) | copy-start | bytes 100
  13.5 208.7 %copy-start.14 = (f32[4,4]{1,0:T(4,128)S(1)}, f32[4,4]{1,0:T(4,128)}, u32[]{:S(2)}) copy-start(f32[4,4]{1,0:T(4,128)} %param.32) | copy-start | bytes 196
  13.6 300.8 %copy-start.11 = (f32[1,256,256]{2,1,0:T(8,128)S(1)}, f32[1,256,256]{2,1,0:T(8,128)}, u32[]{:S(2)}) copy-start(f32[1,256,256]{2,1,0:T(8,128)} %param.27) | copy-start | bytes 786436
  13.6 300.8 %copy-start.15 = (f32[4]{0:T(128)S(1)}, f32[4]{0:T(128)}, u32[]{:S(2)}) copy-start(f32[4]{0:T(128)} %param.31) | copy-start | bytes 52
  13.6 269.5 %reduce-scatter.9.cloned.1.call-start = ((), (), s32[]{:S(2)}) async-start(), calls=%async_computation.12 | async-start | bytes 294912 | tf_op jit(solution)/shard_map/reduce_scatter | solution.py:104
  15.3 313.9 %all-gather.5.cloned.1.call-start = ((), (), s32[]{:S(2)}) async-start(), calls=%async_computation.11 | async-start | bytes 1843200 | tf_op jit(solution)/shard_map/all_gather | solution.py:109
  79.4 295.5 %all-gather.7.cloned.1.call-start = ((), (), s32[]{:S(2)}) async-start(), calls=%async_computation.15 | async-start | bytes 1843200 | tf_op jit(solution)/shard_map/all_gather | solution.py:111
  147.6 280.5 %all-gather.9.cloned.1.call-start = ((), (), s32[]{:S(2)}) async-start(), calls=%async_computation.17 | async-start | bytes 2654208 | tf_op jit(solution)/shard_map/all_gather | solution.py:112
  219.1 377.4 %all-reduce.4.cloned.1.call-start = ((), (), s32[]{:S(2)}) async-start(), calls=%async_computation.20 | async-start | bytes 5898240 | tf_op jit(solution)/shard_map/psum | solution.py:15
  361.4 13.5 %copy-start.1 = (bf16[640,640]{1,0:T(8,128)(2,1)}, bf16[640,640]{1,0:T(8,128)(2,1)S(1)}, u32[]{:S(2)}) copy-start(bf16[640,640]{1,0:T(8,128)(2,1)S(1)} %get-tuple-element.308) | copy-start | bytes 2457604
  437.9 5.9 copy-start.4
  438.0 231.9 %reduce-scatter.11.cloned.1.call-start = ((), (), s32[]{:S(2)}) async-start(), calls=%async_computation.13 | async-start | bytes 2949120 | tf_op jit(solution)/shard_map/reduce_scatter | solution.py:77
  445.8 0.9 copy-start.3
  445.8 371.3 %reduce-scatter.17.cloned.1.call-start = ((), (), s32[]{:S(2)}) async-start(), calls=%async_computation.19 | async-start | bytes 8847360 | tf_op jit(solution)/shard_map/reduce_scatter | solution.py:89
  459.7 395.6 %all-gather.11.cloned.1.call-start = ((), (), s32[]{:S(2)}) async-start(), calls=%async_computation.18 | async-start | bytes 5898240 | tf_op jit(solution)/shard_map/all_gather | solution.py:134
  596.5 79.5 %copy-start.12 = (bf16[1,256,256]{2,1,0:T(8,128)(2,1)S(1)}, bf16[1,256,256]{2,1,0:T(8,128)(2,1)}, u32[]{:S(2)}) copy-start(bf16[1,256,256]{2,1,0:T(8,128)(2,1)} %get-tuple-element.283) | copy-start | bytes 393220
  671.5 12.7 %all-to-all-start.1 = ((bf16[80,8,128]{2,0,1:T(8,128)(2,1)}), bf16[80,8,128]{2,0,1:T(8,128)(2,1)S(1)}, u32[]{:S(2)}, u32[]{:S(2)}) async-start(bf16[80,8,128]{2,0,1:T(8,128)(2,1)} %copy_bitcast_fusion.1), calls=%async_computation.4 | async-start | bytes 327680 | tf_op jit(solution)/shard_map/all_to_all | solution.py:142
  684.2 135.0 %all-to-all-start = ((bf16[80,8,128]{2,0,1:T(8,128)(2,1)}), bf16[80,8,128]{2,0,1:T(8,128)(2,1)S(1)}, u32[]{:S(2)}, u32[]{:S(2)}) async-start(bf16[80,8,128]{2,0,1:T(8,128)(2,1)} %copy.34), calls=%async_computation.3 | async-start | bytes 327680 | tf_op jit(solution)/shard_map/all_to_all | solution.py:141
  819.2 39.4 %copy-start.7 = (bf16[80,8,128]{2,0,1:T(8,128)(2,1)}, bf16[80,8,128]{2,0,1:T(8,128)(2,1)S(1)}, u32[]{:S(2)}) copy-start(bf16[80,8,128]{2,0,1:T(8,128)(2,1)S(1)} %all-to-all-done) | copy-start | bytes 491524
  819.2 40.6 %all-to-all-start.3 = ((bf16[80,8,384]{2,0,1:T(8,128)(2,1)}), bf16[80,8,384]{2,0,1:T(8,128)(2,1)S(1)}, u32[]{:S(2)}, u32[]{:S(2)}) async-start(bf16[80,8,384]{2,0,1:T(8,128)(2,1)} %bitcast.140), calls=%async_computation.9 | async-start | bytes 983040 | tf_op jit(solution)/shard_map/all_to_all | solution.py:144
  858.9 7.2 copy-start.6
  859.0 7.0 copy-start.8
  859.9 19.7 %all-to-all-start.2 = ((bf16[80,8,384]{2,0,1:T(8,128)(2,1)}), bf16[80,8,384]{2,0,1:T(8,128)(2,1)S(1)}, u32[]{:S(2)}, u32[]{:S(2)}) async-start(bf16[80,8,384]{2,0,1:T(8,128)(2,1)} %copy.38), calls=%async_computation.8 | async-start | bytes 983040 | tf_op jit(solution)/shard_map/all_to_all | solution.py:143
  867.0 55.3 %copy-start.5 = (f32[640,384]{1,0:T(8,128)S(1)}, f32[640,384]{1,0:T(8,128)}, u32[]{:S(2)}) copy-start(f32[640,384]{1,0:T(8,128)} %param.34) | copy-start | bytes 2949124
  882.1 41.3 %copy-start.10 = (f32[640,128]{1,0:T(8,128)S(1)}, f32[640,128]{1,0:T(8,128)}, u32[]{:S(2)}) copy-start(f32[640,128]{1,0:T(8,128)} %param.33) | copy-start | bytes 983044
Sparse Core Ops, SparseCore 0:
  11.5 67.9 reduce-scatter.6
  83.2 64.3 reduce-scatter.12
  151.1 67.9 reduce-scatter.14
  222.9 60.2 reduce-scatter.8
  285.2 44.0 all-gather.4
  331.3 43.5 all-gather.6
  377.1 50.9 all-gather.8
  438.1 158.3 all-reduce.3
  600.4 69.3 reduce-scatter.10
  673.8 143.3 reduce-scatter.16
  818.8 36.5 all-gather.10
where the time goes:
time: 936 us; the launch traced here: 931 us
  waiting for transfers between devices  714 us (76%)
  blocking collectives  91.5 us (10%)
  matrix products  42.8 us (5%)
  starting transfers between devices  19.2 us (2%)
  between operations  19.1 us (2%)
  loops' own time  16.7 us (2%)
  other arithmetic  15.2 us (2%)
  local copies, waits for them, and re-layouts  12 us (1%)
    psum x1, waiting for transfers between devices, spread(): return lax.psum(jnp.where(mine, value, jnp.zeros_like(value)), axis)  137 us
    reduce_scatter x1, waiting for transfers between devices, shards(): lax.psum_scatter(lax.dot_general(column_block, full_up, (((0,), (0,)), ((...  127 us
    reduce_scatter x1, waiting for transfers between devices, shards(): lax.psum_scatter(lax.dot_general(column_block, full_kv, (((0,), (0,)), ((...  73.3 us
    reduce_scatter x1, waiting for transfers between devices, shards(): lax.psum_scatter(partials[3], 'dp', scatter_dimension=0, tiled=True)  71.4 us
    reduce_scatter x1, waiting for transfers between devices, shards(): lax.psum_scatter(partials[2], 'dp', scatter_dimension=0, tiled=True)  68.1 us
    reduce_scatter x1, waiting for transfers between devices, shards(): lax.psum_scatter(partials[0], 'dp', scatter_dimension=0, tiled=True)  64 us
    reduce_scatter x1, waiting for transfers between devices, shards(): lax.psum_scatter(partials[1], 'dp', scatter_dimension=0, tiled=True)  59.8 us
    all_gather x1, waiting for transfers between devices, shards(): lax.all_gather(summed_rows[3], 'dp', axis=0, tiled=True)  41.4 us
  transfers between devices with their start and end apart: 15, of which 12 were waited for; matrix products, arithmetic and copies ran while one was open for 6% of the time, Pallas kernels for 0%

commit v1 on v0

--- a/solution.py
+++ b/solution.py
@@ -8,6 +8,18 @@
 OUT_UP = 3072
 NF = 4
 NS_STEPS = 2
+
+
+def doubled_up(x, axis, dim):
+    ways, here = (lax.axis_size(axis), lax.axis_index(axis))
+    grown, reach = (x, 1)
+    while reach < ways:
+        theirs = lax.ppermute(grown, axis, [(d, d ^ reach) for d in range(ways)])
+        mine_first = jnp.concatenate([grown, theirs], axis=dim)
+        theirs_first = jnp.concatenate([theirs, grown], axis=dim)
+        grown = jnp.where(here & reach == 0, mine_first, theirs_first)
+        reach = 2 * reach
+    return grown
 
 
 def spread(value, axis, root):
@@ -131,7 +143,7 @@
         inverses.append(spread(local_inverse, "dp", owner_index))
     blocks_kv, blocks_up = (
         lax.all_gather(inverses[1][None], "own", axis=0, tiled=True),
-        lax.all_gather(inverses[3][None], "own", axis=0, tiled=True),
+        doubled_up(inverses[3][None], "own", 0),
     )
     low_kv = gradient_kv.astype(jnp.bfloat16)
     low_up = gradient_up.astype(jnp.bfloat16)

time: 936 us -> 916 us (0.979)
  waiting for transfers between devices: 714 us -> 693 us
    all_gather x1 -> x0, waiting for transfers between devices: 32.4 us -> none  [shards(): lax.all_gather(inverses[3][None], 'own', axis=0, tiled=True)]
    all_to_all x1, waiting for transfers between devices: 0.01 us -> 11.9 us  [shards(): lax.all_to_all(low_up, 'dp', split_axis=1, concat_axis=0, tiled=True)]
  transfers between devices with their start and end apart: 15 -> 16, of which waited for: 12 -> 14; matrix products, arithmetic and copies ran while one was open for 6% -> 7% of each run, Pallas kernels for 0% -> 0%
where the time goes in v1:
time: 916 us; the launch traced here: 911 us
  waiting for transfers between devices  693 us (76%)
  blocking collectives  91.5 us (10%)
  matrix products  43.7 us (5%)
  between operations  19.3 us (2%)
  other arithmetic  18 us (2%)
  loops' own time  16.8 us (2%)
  starting transfers between devices  16.5 us (2%)
  local copies, waits for them, and re-layouts  12 us (1%)
    psum x1, waiting for transfers between devices, spread(): return lax.psum(jnp.where(mine, value, jnp.zeros_like(value)), axis)  137 us
    reduce_scatter x1, waiting for transfers between devices, shards(): lax.psum_scatter(lax.dot_general(column_block, full_up, (((0,), (0,)), ((...  128 us
    reduce_scatter x1, waiting for transfers between devices, shards(): lax.psum_scatter(partials[3], 'dp', scatter_dimension=0, tiled=True)  71.4 us
    reduce_scatter x1, waiting for transfers between devices, shards(): lax.psum_scatter(partials[2], 'dp', scatter_dimension=0, tiled=True)  68.1 us
    reduce_scatter x1, waiting for transfers between devices, shards(): lax.psum_scatter(lax.dot_general(column_block, full_kv, (((0,), (0,)), ((...  65.4 us
    reduce_scatter x1, waiting for transfers between devices, shards(): lax.psum_scatter(partials[0], 'dp', scatter_dimension=0, tiled=True)  64 us
    reduce_scatter x1, waiting for transfers between devices, shards(): lax.psum_scatter(partials[1], 'dp', scatter_dimension=0, tiled=True)  59.7 us
    all_gather x1, waiting for transfers between devices, shards(): lax.all_gather(summed_rows[3], 'dp', axis=0, tiled=True)  41.5 us
  transfers between devices with their start and end apart: 16, of which 14 were waited for; matrix products, arithmetic and copies ran while one was open for 7% of the time, Pallas kernels for 0%

profile of v1, /device:TPU:0, one launch (start us, length us, event | category | flops | bytes accessed | tf_op | source)
XLA Modules:
  0.0 911.2 jit_solution(1075256479477026969)
XLA Ops:
  15.4 64.0 %reduce-scatter.7.cloned.1.call-done = f32[80,640]{1,0:T(8,128)} async-done(((f32[640,640]{1,0:T(8,128)}), f32[80,640]{1,0:T(8,128)}) %reduce-scatter.7.cloned.1.call-update) | async-done | bytes 204816 | tf_op jit(solution)/shard_map/reduce_scatter | solution.py:115
  79.5 68.1 %reduce-scatter.13.cloned.1.call-done = f32[80,640]{1,0:T(8,128)} async-done(((f32[640,640]{1,0:T(8,128)}), f32[80,640]{1,0:T(8,128)}) %reduce-scatter.13.cloned.1.call-update) | async-done | bytes 204816 | tf_op jit(solution)/shard_map/reduce_scatter | solution.py:117
  147.7 71.4 %reduce-scatter.15.cloned.1.call-done = f32[96,768]{1,0:T(8,128)} async-done(((f32[768,768]{1,0:T(8,128)}), f32[96,768]{1,0:T(8,128)}) %reduce-scatter.15.cloned.1.call-update) | async-done | bytes 294928 | tf_op jit(solution)/shard_map/reduce_scatter | solution.py:118
  223.4 59.7 %reduce-scatter.9.cloned.1.call-done = f32[32,256]{1,0:T(8,128)} async-done(((f32[256,256]{1,0:T(8,128)}), f32[32,256]{1,0:T(8,128)}) %reduce-scatter.9.cloned.1.call-update) | async-done | bytes 32784 | tf_op jit(solution)/shard_map/reduce_scatter | solution.py:116
  283.1 31.2 %all_gather.22 = f32[256,256]{1,0:T(8,128)S(1)} all-gather(f32[32,256]{1,0:T(8,128)} %reduce-scatter.9.cloned.1.call-done), channel_id=1, replica_groups=mesh['dp'=8,'own'=4] {'dp'}, dimensions={0}, use_global_device_ids=true | all-gather | bytes 294912 | tf_op jit(solution)/shard_map/all_gather | solution.py:122
  315.1 14.1 %all-gather.4.cloned.1.call-done = f32[640,640]{1,0:T(8,128)} async-done(((f32[80,640]{1,0:T(8,128)}), f32[640,640]{1,0:T(8,128)}) %all-gather.4.cloned.1.call-update) | async-done | bytes 1638416 | tf_op jit(solution)/shard_map/all_gather | solution.py:121
  332.0 29.3 %conditional.4 = (bf16[640,640]{1,0:T(8,128)(2,1)S(1)}) conditional(s32[]{:T(128)} %convert_element_type.80, () %tuple.44, (f32[4]{0:T(128)S(1)}, s32[2,4]{1,0:T(2,128)S(1)}, f32[1,640,640]{2,1,0:T(8,128)}, f32[640,640]{1,0:T(8,128)S(1)}, f32[640,640]{1,0:T(8,128)}, /*index=5*/f32[640,640]{1,0:T(8,128)}, f32[4]{0:T(128)S(1)}, ...), branch_computations={%region_1.0_spmd, %region_2.0_spmd} | conditional | flops 12590694400 | bytes 25804862 | solution.py:137
  333.3 4.2 multiply_reduce_fusion
  338.2 4.6 fusion.2
  342.8 4.7 fusion.4
  347.5 8.3 fusion.79
  355.8 5.1 subtract_convert_fusion
  361.3 13.6 %all-gather.6.cloned.1.call-done = f32[640,640]{1,0:T(8,128)} async-done(((f32[80,640]{1,0:T(8,128)}), f32[640,640]{1,0:T(8,128)}) %all-gather.6.cloned.1.call-update) | async-done | bytes 1638416 | tf_op jit(solution)/shard_map/all_gather | solution.py:123
  374.9 9.1 conditional.6
  386.5 41.5 %all-gather.8.cloned.1.call-done = f32[768,768]{1,0:T(8,128)} async-done(((f32[96,768]{1,0:T(8,128)}), f32[768,768]{1,0:T(8,128)}) %all-gather.8.cloned.1.call-update) | async-done | bytes 2359312 | tf_op jit(solution)/shard_map/all_gather | solution.py:124
  431.3 5.9 conditional.7
  438.4 5.8 all_gather.24
  447.2 8.7 all_gather.27
  455.9 4.3 fusion.88
  460.2 136.6 %all-reduce.4.cloned.1.call-done = (bf16[640,640]{1,0:T(8,128)(2,1)}, bf16[1,256,256]{2,1,0:T(8,128)(2,1)}, bf16[640,640]{1,0:T(8,128)(2,1)}, bf16[1,768,768]{2,1,0:T(8,128)(2,1)}) async-done(((bf16[640,640]{1,0:T(8,128)(2,1)}, bf16[1,256,256]{2,1,0:T(8,128)(2,1)}, bf16[640,640]{1,0:T(8,128)(2,1)}, bf16[1,768,768]{2,1,0:T(8,128)(2,1)}), (bf16[640,640]{1,0:T(8,128)(2,1)}, bf16[1,256,256]{2,1,0:T(8,128)(2,1)}, ...) | async-done | bytes 2949136 | tf_op jit(solution)/shard_map/psum | solution.py:27
  596.8 3.2 collective-permute-done
  604.4 65.4 %reduce-scatter.11.cloned.1.call-done = f32[80,1024]{1,0:T(8,128)} async-done(((f32[640,1024]{1,0:T(8,128)}), f32[80,1024]{1,0:T(8,128)}) %reduce-scatter.11.cloned.1.call-update) | async-done | bytes 327696 | tf_op jit(solution)/shard_map/reduce_scatter | solution.py:89
  671.5 3.5 all-to-all-start.1
  676.0 7.2 all_gather.23
  684.3 128.4 %reduce-scatter.17.cloned.1.call-done = f32[80,3072]{1,0:T(8,128)} async-done(((f32[640,3072]{1,0:T(8,128)}), f32[80,3072]{1,0:T(8,128)}) %reduce-scatter.17.cloned.1.call-update) | async-done | bytes 983056 | tf_op jit(solution)/shard_map/reduce_scatter | solution.py:101
  813.9 3.7 all-to-all-start
  817.7 3.9 fusion.65
  825.3 3.7 all-to-all-start.2
  829.8 12.6 %all-to-all-done.2 = bf16[80,8,384]{2,0,1:T(8,128)(2,1)S(1)} async-done(((bf16[80,8,384]{2,0,1:T(8,128)(2,1)}), bf16[80,8,384]{2,0,1:T(8,128)(2,1)S(1)}, u32[]{:S(2)}, u32[]{:S(2)}) %all-to-all-start.2) | async-done | bytes 491552 | tf_op jit(solution)/shard_map/all_to_all | solution.py:155
  842.4 3.6 all-to-all-start.3
  847.7 11.9 %all-to-all-done.3 = bf16[80,8,384]{2,0,1:T(8,128)(2,1)S(1)} async-done(((bf16[80,8,384]{2,0,1:T(8,128)(2,1)}), bf16[80,8,384]{2,0,1:T(8,128)(2,1)S(1)}, u32[]{:S(2)}, u32[]{:S(2)}) %all-to-all-start.3) | async-done | bytes 491552 | tf_op jit(solution)/shard_map/all_to_all | solution.py:156
  862.1 38.7 %all-reduce = (f32[]{:T(128)}, f32[]{:T(128)}) all-reduce(f32[]{:T(128)} %get-tuple-element.298, f32[]{:T(128)} %get-tuple-element.300), channel_id=1, replica_groups=mesh['dp'=8,'own'=4] {'dp','own'}, use_global_device_ids=true, to_apply=%region_12.13 | all-reduce | flops 2 | bytes 16 | tf_op jit(solution)/shard_map/psum | solution.py:162
  (92 shorter events, 43.3 us)
Async XLA Ops:
  7.2 2.8 copy-start
  7.2 72.2 %reduce-scatter.7.cloned.1.call-start = ((), (), s32[]{:S(2)}) async-start(), calls=%async_computation.10 | async-start | bytes 1843200 | tf_op jit(solution)/shard_map/reduce_scatter | solution.py:115
  9.9 1.7 copy-start.2
  9.9 137.7 %reduce-scatter.13.cloned.1.call-start = ((), (), s32[]{:S(2)}) async-start(), calls=%async_computation.14 | async-start | bytes 1843200 | tf_op jit(solution)/shard_map/reduce_scatter | solution.py:117
  11.6 207.5 %reduce-scatter.15.cloned.1.call-start = ((), (), s32[]{:S(2)}) async-start(), calls=%async_computation.16 | async-start | bytes 2654208 | tf_op jit(solution)/shard_map/reduce_scatter | solution.py:118
  13.6 0.8 copy-start.7
  13.6 205.6 %copy-start.11 = (s32[2,4]{1,0:T(2,128)S(1)}, s32[2,4]{1,0:T(2,128)}, u32[]{:S(2)}) copy-start(s32[2,4]{1,0:T(2,128)} %param.30) | copy-start | bytes 100
  13.6 208.7 %copy-start.12 = (f32[4,4]{1,0:T(4,128)S(1)}, f32[4,4]{1,0:T(4,128)}, u32[]{:S(2)}) copy-start(f32[4,4]{1,0:T(4,128)} %param.32) | copy-start | bytes 196
  13.6 300.7 %copy-start.9 = (f32[1,256,256]{2,1,0:T(8,128)S(1)}, f32[1,256,256]{2,1,0:T(8,128)}, u32[]{:S(2)}) copy-start(f32[1,256,256]{2,1,0:T(8,128)} %param.27) | copy-start | bytes 786436
  13.6 300.7 %copy-start.13 = (f32[4]{0:T(128)S(1)}, f32[4]{0:T(128)}, u32[]{:S(2)}) copy-start(f32[4]{0:T(128)} %param.31) | copy-start | bytes 52
  13.6 269.5 %reduce-scatter.9.cloned.1.call-start = ((), (), s32[]{:S(2)}) async-start(), calls=%async_computation.12 | async-start | bytes 294912 | tf_op jit(solution)/shard_map/reduce_scatter | solution.py:116
  15.4 313.8 %all-gather.4.cloned.1.call-start = ((), (), s32[]{:S(2)}) async-start(), calls=%async_computation.11 | async-start | bytes 1843200 | tf_op jit(solution)/shard_map/all_gather | solution.py:121
  79.4 295.5 %all-gather.6.cloned.1.call-start = ((), (), s32[]{:S(2)}) async-start(), calls=%async_computation.15 | async-start | bytes 1843200 | tf_op jit(solution)/shard_map/all_gather | solution.py:123
  147.6 280.4 %all-gather.8.cloned.1.call-start = ((), (), s32[]{:S(2)}) async-start(), calls=%async_computation.17 | async-start | bytes 2654208 | tf_op jit(solution)/shard_map/all_gather | solution.py:124
  219.1 377.6 %all-reduce.4.cloned.1.call-start = ((), (), s32[]{:S(2)}) async-start(), calls=%async_computation.19 | async-start | bytes 5898240 | tf_op jit(solution)/shard_map/psum | solution.py:27
  361.3 13.6 %copy-start.1 = (bf16[640,640]{1,0:T(8,128)(2,1)}, bf16[640,640]{1,0:T(8,128)(2,1)S(1)}, u32[]{:S(2)}) copy-start(bf16[640,640]{1,0:T(8,128)(2,1)S(1)} %get-tuple-element.308) | copy-start | bytes 2457604
  438.3 5.9 copy-start.4
  438.3 231.5 %reduce-scatter.11.cloned.1.call-start = ((), (), s32[]{:S(2)}) async-start(), calls=%async_computation.13 | async-start | bytes 2949120 | tf_op jit(solution)/shard_map/reduce_scatter | solution.py:89
  446.3 0.9 copy-start.3
  446.3 366.4 %reduce-scatter.17.cloned.1.call-start = ((), (), s32[]{:S(2)}) async-start(), calls=%async_computation.18 | async-start | bytes 8847360 | tf_op jit(solution)/shard_map/reduce_scatter | solution.py:101
  596.7 3.2 collective-permute-start
  596.8 79.3 %copy-start.10 = (bf16[1,256,256]{2,1,0:T(8,128)(2,1)S(1)}, bf16[1,256,256]{2,1,0:T(8,128)(2,1)}, u32[]{:S(2)}) copy-start(bf16[1,256,256]{2,1,0:T(8,128)(2,1)} %get-tuple-element.283) | copy-start | bytes 393220
  602.8 214.8 %collective-permute-start.1 = (bf16[2,768,768]{2,1,0:T(8,128)(2,1)S(1)}, bf16[2,768,768]{2,1,0:T(8,128)(2,1)}, u32[]{:S(2)}, u32[]{:S(2)}) collective-permute-start(bf16[2,768,768]{2,1,0:T(8,128)(2,1)S(1)} %maximum_select_fusion.2), channel_id=1, source_target_pairs={{0,2},{1,3},{2,0},{3,1},{4,6},{5,7},{6,4},{7,5},{8,10},{9,11},{10,... | collective-permute-start | bytes 7077896 | tf_op jit(solution)/shard_map/ppermute | solution.py:17
  671.5 142.4 %all-to-all-start.1 = ((bf16[80,8,128]{2,0,1:T(8,128)(2,1)}), bf16[80,8,128]{2,0,1:T(8,128)(2,1)S(1)}, u32[]{:S(2)}, u32[]{:S(2)}) async-start(bf16[80,8,128]{2,0,1:T(8,128)(2,1)} %copy_bitcast_fusion.1), calls=%async_computation.4 | async-start | bytes 327680 | tf_op jit(solution)/shard_map/all_to_all | solution.py:154
  813.9 11.4 %all-to-all-start = ((bf16[80,8,128]{2,0,1:T(8,128)(2,1)}), bf16[80,8,128]{2,0,1:T(8,128)(2,1)S(1)}, u32[]{:S(2)}, u32[]{:S(2)}) async-start(bf16[80,8,128]{2,0,1:T(8,128)(2,1)} %copy.34), calls=%async_computation.3 | async-start | bytes 327680 | tf_op jit(solution)/shard_map/all_to_all | solution.py:153
  822.9 23.8 %copy-start.6 = (bf16[640,640]{1,0:T(8,128)(2,1)S(1)}, bf16[640,640]{1,0:T(8,128)(2,1)}, u32[]{:S(2)}) copy-start(bf16[640,640]{1,0:T(8,128)(2,1)} %get-tuple-element.282) | copy-start | bytes 2457604
  825.3 17.1 %all-to-all-start.2 = ((bf16[80,8,384]{2,0,1:T(8,128)(2,1)}), bf16[80,8,384]{2,0,1:T(8,128)(2,1)S(1)}, u32[]{:S(2)}, u32[]{:S(2)}) async-start(bf16[80,8,384]{2,0,1:T(8,128)(2,1)} %copy.38), calls=%async_computation.8 | async-start | bytes 983040 | tf_op jit(solution)/shard_map/all_to_all | solution.py:155
  842.4 17.2 %all-to-all-start.3 = ((bf16[80,8,384]{2,0,1:T(8,128)(2,1)}), bf16[80,8,384]{2,0,1:T(8,128)(2,1)S(1)}, u32[]{:S(2)}, u32[]{:S(2)}) async-start(bf16[80,8,384]{2,0,1:T(8,128)(2,1)} %bitcast.139), calls=%async_computation.9 | async-start | bytes 983040 | tf_op jit(solution)/shard_map/all_to_all | solution.py:156
  847.7 54.6 %copy-start.5 = (f32[640,384]{1,0:T(8,128)S(1)}, f32[640,384]{1,0:T(8,128)}, u32[]{:S(2)}) copy-start(f32[640,384]{1,0:T(8,128)} %param.34) | copy-start | bytes 2949124
  862.1 41.2 %copy-start.8 = (f32[640,128]{1,0:T(8,128)S(1)}, f32[640,128]{1,0:T(8,128)}, u32[]{:S(2)}) copy-start(f32[640,128]{1,0:T(8,128)} %param.33) | copy-start | bytes 983044
Sparse Core Ops, SparseCore 0:
  11.5 67.9 reduce-scatter.6
  83.2 64.3 reduce-scatter.12
  151.1 67.9 reduce-scatter.14
  222.9 60.2 reduce-scatter.8
  285.2 44.0 all-gather.3
  331.3 43.6 all-gather.5
  377.1 50.9 all-gather.7
  438.4 158.2 all-reduce.3
  600.7 69.1 reduce-scatter.10
  673.8 138.8 reduce-scatter.16
